TPU v7x, 256 devices: a whole 4x4x8 slice. The times are simulated.
256 devices in a mesh: seq: 16 (over z, x_hi), mp: 16 (over y, x_lo, core).
Axes of the slice: x: 4 (x_hi: 2, x_lo: 2; x = x_hi * 2 + x_lo), y: 4, z: 8, core: 2. Of those that a mesh axis runs over, the one named last changes fastest.
Arguments:
- tokens: bfloat16 [8192, 4608], P('seq', 'mp')
- pre_gain: bfloat16 [4608], P('mp'), may hold values from -2.5 to 2.5
- post_gain: bfloat16 [4608], P('mp'), may hold values from -2.5 to 2.5
- w_query: bfloat16 [4608, 4096], P('seq', 'mp')
- w_key: bfloat16 [4608, 2048], P('seq', 'mp')
- w_value: bfloat16 [4608, 2048], P('seq', 'mp'), may hold values from -0.09375 to 0.09375
- w_out: bfloat16 [4096, 4608], P('mp', 'seq')
- segment_ids: int32 [8192], P('seq'), may hold values from 0 to 3, never falling along the last dimension, each value on 1 to 6553 neighbouring positions
- page_table: int32 [64], P('seq'), may hold values from 0 to 63, as said below
Outputs:
- layer_output: bfloat16 [8192, 4608], P('seq', 'mp')
- key_cache: bfloat16 [64, 128, 2048], P('seq', None, 'mp')
- value_cache: bfloat16 [64, 128, 2048], P('seq', None, 'mp')
Inputs may be any that keep to these rules, and one draw needn't show every extreme that they name: segment_ids never fall along the stream, every tenant of 0 to 3 is present, each has at least 1 and at most 6553 tokens and one has exactly 6553. page_table is a permutation; the slot of page p lies in the same block of 4 slots as p, that is page_table[p] // 4 = p // 4.
All inputs are finite; a program needn't handle non-finite values.
Results may differ from a plain program's by a relative error of at most 0.019.
Values may be sent and summed in bfloat16 or wider, within the bound.
No kernel may reach another device: no remote copies, remote signals or barrier semaphores. Data moves between devices by JAX's collectives and lax.ppermute only.
A program may use at most 64 MiB of HBM per device.

v0:
```python
import math
import jax
import jax.numpy as jnp
from jax import lax
from jax.sharding import PartitionSpec as P

D = 4608
HQ = 32
HD = 128
WINDOW = 4096
PAGE = 128
SEGS = 4
EPSILON = 1e-06
SOFT_CAP = 50.0
LARGE_INDEX = 1 << 30


def from_behind(block, axis, distance):
    devices = range(lax.axis_size(axis))
    route = [(i - distance, i) for i in devices if i - distance in devices]
    return lax.ppermute(block, axis, route)


def rotate(values, positions):
    half = values.shape[-1] // 2
    freqs = jnp.exp(
        -math.log(10000.0) * jnp.arange(half, dtype=jnp.float32) * (2.0 / values.shape[-1])
    )
    angles = positions.astype(jnp.float32)[:, None] * freqs[None, :]
    cosine = jnp.cos(angles)[:, None, :]
    sine = jnp.sin(angles)[:, None, :]
    first = values[..., :half]
    second = values[..., half:]
    return jnp.concatenate(
        [first * cosine - second * sine, second * cosine + first * sine], axis=-1
    )


def add_product(normed, piece):
    return jnp.dot(normed, piece, preferred_element_type=jnp.float32)


def shards(tokens, pre_gain, post_gain, w_query, w_key, w_value, w_out, segment_ids, page_table):
    rows_here = tokens.shape[0]
    whole, gain_full = (
        lax.all_gather(tokens, "mp", axis=1, tiled=True),
        lax.all_gather(pre_gain, "mp", axis=0, tiled=True),
    )
    x_whole = whole.astype(jnp.float32)
    pre_scale = lax.rsqrt(jnp.mean(x_whole * x_whole, axis=1, keepdims=True) + EPSILON)
    normed = (x_whole * pre_scale * (1.0 + gain_full.astype(jnp.float32))[None, :]).astype(
        jnp.bfloat16
    )
    query_raw = add_product(normed, lax.all_gather(w_query, "seq", axis=0, tiled=True))
    key_raw = add_product(normed, lax.all_gather(w_key, "seq", axis=0, tiled=True))
    value_raw = add_product(normed, lax.all_gather(w_value, "seq", axis=0, tiled=True))
    heads_query = w_query.shape[1] // HD
    heads_kv = w_key.shape[1] // HD
    seq_index = lax.axis_index("seq")
    base = seq_index * rows_here
    global_index = base + jnp.arange(rows_here, dtype=jnp.int32)
    local_first = jnp.stack(
        [jnp.min(jnp.where(segment_ids == s, global_index, LARGE_INDEX)) for s in range(SEGS)]
    )
    starts = lax.pmin(local_first, "seq")
    offsets = jnp.zeros((rows_here,), jnp.int32)
    for s in range(SEGS):
        offsets = offsets + jnp.where(segment_ids == s, starts[s], 0)
    within = global_index - offsets
    query_scale = float(D // HQ) ** (-0.5)
    queries = (rotate(query_raw.reshape(rows_here, heads_query, HD), within) * query_scale).astype(
        jnp.bfloat16
    )
    keys_here = rotate(key_raw.reshape(rows_here, heads_kv, HD), within).astype(jnp.bfloat16)
    values_here = value_raw.reshape(rows_here, heads_kv, HD).astype(jnp.bfloat16)
    reach = WINDOW // rows_here
    earlier = []
    current = (keys_here, values_here)
    for distance in range(reach):
        current = from_behind((current[0], current[1]), "seq", 1)
        earlier.append(current)
    earlier = earlier[::-1]
    keys_all = jnp.concatenate([pair[0] for pair in earlier] + [keys_here], axis=0)
    values_all = jnp.concatenate([pair[1] for pair in earlier] + [values_here], axis=0)
    block = math.gcd(rows_here, 512)
    grouped = queries.reshape(rows_here, heads_kv, heads_query // heads_kv, HD)

    def attend(start):
        query_pos = base + start + jnp.arange(block, dtype=jnp.int32)
        key_pos = base - WINDOW + start + jnp.arange(WINDOW + block, dtype=jnp.int32)
        key_segment = jnp.zeros((WINDOW + block,), jnp.int32)
        for s in range(1, SEGS):
            key_segment = key_segment + (key_pos >= starts[s]).astype(jnp.int32)
        distance = query_pos[:, None] - key_pos[None, :]
        allowed = (
            (key_pos >= 0)[None, :]
            & (distance >= 0)
            & (distance < WINDOW)
            & (segment_ids[:, None] == key_segment[None, :])
        )
        scores = jnp.einsum("qgrd,kgd->grqk", grouped, keys_all, preferred_element_type=jnp.float32)
        capped = SOFT_CAP * jnp.tanh(scores / SOFT_CAP)
        weights = jnp.where(allowed[None, None], jnp.exp(capped), 0.0)
        denominator = jnp.sum(weights, axis=-1)
        rounded = weights.astype(jnp.bfloat16)
        summed = jnp.einsum(
            "grqk,kgd->qgrd", rounded, values_all, preferred_element_type=jnp.float32
        )
        result = summed / jnp.transpose(denominator, (2, 0, 1))[..., None]
        return result.astype(jnp.bfloat16).reshape(block, heads_query * HD)

    block_starts = jnp.arange(rows_here // block, dtype=jnp.int32) * block
    attended = lax.map(attend, block_starts).reshape(rows_here, heads_query * HD)
    group_terms = jnp.dot(
        attended,
        lax.all_gather(w_out, "seq", axis=1, tiled=True),
        preferred_element_type=jnp.float32,
    )
    attention_share = lax.psum_scatter(
        group_terms.astype(jnp.bfloat16), "mp", scatter_dimension=1, tiled=True
    ).astype(jnp.float32)
    squares = jnp.sum(attention_share * attention_share, axis=1)
    square_total = lax.psum(squares, "mp")
    post_scale = lax.rsqrt(square_total / D + EPSILON)
    post = attention_share * post_scale[:, None] * (1.0 + post_gain.astype(jnp.float32))[None, :]
    layer_output = (tokens.astype(jnp.float32) + post).astype(jnp.bfloat16)
    pages_here = page_table.shape[0]
    local_slot = page_table - seq_index * pages_here
    one_hot = (local_slot[None, :] == jnp.arange(pages_here, dtype=jnp.int32)[:, None]).astype(
        jnp.bfloat16
    )
    stacked = jnp.stack(
        [
            keys_here.reshape(pages_here, PAGE, heads_kv * HD),
            values_here.reshape(pages_here, PAGE, heads_kv * HD),
        ]
    )
    placed = jnp.einsum(
        "sp,tpce->tsce", one_hot, stacked, preferred_element_type=jnp.float32
    ).astype(jnp.bfloat16)
    return (layer_output, placed[0], placed[1])


def solution(mesh):
    return jax.shard_map(
        shards,
        mesh=mesh,
        in_specs=(
            P("seq", "mp"),
            P("mp"),
            P("mp"),
            P("seq", "mp"),
            P("seq", "mp"),
            P("seq", "mp"),
            P("mp", "seq"),
            P("seq"),
            P("seq"),
        ),
        out_specs=(P("seq", "mp"), P("seq", None, "mp"), P("seq", None, "mp")),
        check_vma=False,
    )
```

profile of v0, /device:TPU:32, one launch (start us, length us, event | category | flops | bytes accessed | tf_op | source)
XLA Modules:
  0.0 506.7 jit_solution(7526832199181364429)
XLA Ops:
  7.2 0.7 all-gather.6.cloned.1.call-update
  7.9 0.7 all-gather.10.cloned.1.call-update
  8.7 0.7 all-gather.8.cloned.1.call-update
  9.4 0.5 all-gather.12.cloned.1.call-update
  10.0 1.4 select_reduce_fusion.3
  11.4 2.6 pad_add_fusion
  14.0 19.3 %pmin.7 = s32[4]{0:T(128)S(1)} all-reduce(s32[4]{0:T(128)S(1)} %pad_add_fusion), channel_id=1, replica_groups=mesh['seq'=16,'mp'=16] {'seq'}, use_global_device_ids=true, to_apply=%region_5.6 | all-reduce | flops 4 | bytes 32 | tf_op jit(solution)/shard_map/pmin | solution.py:65
  33.3 1.3 dynamic-slice
  35.2 0.9 dynamic-update-slice
  36.1 53.1 %all-reduce = bf16[4608]{0:T(1024)(128)(2,1)S(1)} all-reduce(bf16[4608]{0:T(1024)(128)(2,1)S(1)} %dynamic-update-slice), channel_id=1, replica_groups=mesh['seq'=16,'mp'=16] {'mp'}, use_global_device_ids=true, to_apply=%add | all-reduce | flops 4608 | bytes 18432
  89.2 0.7 fusion.67
  89.8 2.6 subtract_convert_fusion
  92.5 3.4 fusion.2
  95.9 39.3 %all-gather.10.cloned.1.call-done = bf16[4608,128]{1,0:T(8,128)(2,1)} async-done(((bf16[288,128]{1,0:T(8,128)(2,1)}), bf16[4608,128]{1,0:T(8,128)(2,1)}) %all-gather.10.cloned.1.call-update) | async-done | bytes 1179664 | tf_op jit(solution)/shard_map/all_gather | solution.py:55
  135.2 4.4 convolution_bitcast_fusion
  139.6 0.6 fusion.46
  140.2 2.5 collective-permute-start.8
  142.7 71.6 %all-gather.8.cloned.1.call-done = bf16[4608,128]{1,0:T(8,128)(2,1)} async-done(((bf16[288,128]{1,0:T(8,128)(2,1)}), bf16[4608,128]{1,0:T(8,128)(2,1)}) %all-gather.8.cloned.1.call-update) | async-done | bytes 1179664 | tf_op jit(solution)/shard_map/all_gather | solution.py:56
  214.3 4.8 convolution_convert_fusion.2
  219.2 2.5 collective-permute-start
  221.7 5.4 %collective-permute-start.9 = (bf16[512,1,128]{0,2,1:T(8,128)(2,1)S(1)}, bf16[512,1,128]{0,2,1:T(8,128)(2,1)S(1)}, u32[]{:S(2)}, u32[]{:S(2)}) collective-permute-start(bf16[512,1,128]{0,2,1:T(8,128)(2,1)S(1)} %collective-permute-done.8), channel_id=1, source_target_pairs={{0,16},{16,32},{32,48},{48,64},{64,80},{80,96},{96,112},{112,128},... | collective-permute-start | bytes 393224 | tf_op jit(solution)/shard_map/ppermute | solution.py:21
  227.2 1.2 collective-permute-done
  228.4 2.7 collective-permute-start.1
  231.2 0.9 collective-permute-done.9
  232.1 4.3 collective-permute-start.10
  236.4 2.0 convert_add_fusion
  238.4 2.9 collective-permute-start.2
  241.3 2.2 collective-permute-done.10
  243.5 3.7 collective-permute-start.11
  247.3 5.2 %fusion.10 = pred[512,4608]{0,1:T(8,128)(4,1)S(1)} fusion(s32[512]{0:T(512)S(1)} %copy-done.21, s32[4608]{0:T(1024)S(1)} %get-tuple-element.61, s32[512]{0:T(512)S(1)} %iota_add_fusion.1, s32[4608]{0:T(1024)S(1)} %get-tuple-element.60, pred[4608]{0:T(1024)(128)(4,1)S(1)} %fusion.52), kind=kLoop, calls=%fused_computation.14 | loop fusion | flops 16515072 | bytes 2404864 | tf_op jit(solution)/shard_map/while/body/eval_jaxpr/and | solution.py:96
  252.5 4.0 collective-permute-start.3
  256.5 4.7 collective-permute-start.12
  261.1 1.8 multiply_cosine_fusion
  263.0 4.3 collective-permute-start.4
  267.3 4.3 collective-permute-start.13
  271.7 32.8 %all-gather.12.cloned.1.call-done = bf16[4608,256]{1,0:T(8,128)(2,1)} async-done(((bf16[288,256]{1,0:T(8,128)(2,1)}), bf16[4608,256]{1,0:T(8,128)(2,1)}) %all-gather.12.cloned.1.call-update) | async-done | bytes 2359312 | tf_op jit(solution)/shard_map/all_gather | solution.py:54
  304.5 4.9 fusion.62
  309.4 2.4 collective-permute-start.5
  311.8 5.1 %collective-permute-start.14 = (bf16[512,1,128]{0,2,1:T(8,128)(2,1)}, bf16[512,1,128]{0,2,1:T(8,128)(2,1)}, u32[]{:S(2)}, u32[]{:S(2)}) collective-permute-start(bf16[512,1,128]{0,2,1:T(8,128)(2,1)} %collective-permute-done.13), channel_id=1, source_target_pairs={{0,16},{16,32},{32,48},{48,64},{64,80},{80,96},{96,112},{112,128},... | collective-permute-start | bytes 393224 | tf_op jit(solution)/shard_map/ppermute | solution.py:21
  316.9 0.8 fusion.66
  317.8 1.1 copy.28
  319.1 2.4 collective-permute-start.6
  321.5 0.7 collective-permute-done.14
  322.2 6.0 %collective-permute-start.15 = (bf16[512,1,128]{0,2,1:T(8,128)(2,1)}, bf16[512,1,128]{0,2,1:T(8,128)(2,1)S(1)}, u32[]{:S(2)}, u32[]{:S(2)}) collective-permute-start(bf16[512,1,128]{0,2,1:T(8,128)(2,1)} %collective-permute-done.14), channel_id=1, source_target_pairs={{0,16},{16,32},{32,48},{48,64},{64,80},{80,96},{96,112},{112,128},... | collective-permute-start | bytes 393224 | tf_op jit(solution)/shard_map/ppermute | solution.py:21
  328.2 1.1 multiply_subtract_fusion
  329.4 2.7 collective-permute-start.7
  332.2 1.0 collective-permute-done.15
  333.1 0.9 constant_dynamic-update-slice_fusion.16
  334.1 0.9 constant_dynamic-update-slice_fusion.15
  335.1 4.2 collective-permute-done.7
  339.4 0.9 constant_dynamic-update-slice_fusion.6
  340.3 0.9 constant_dynamic-update-slice_fusion.5
  341.4 6.7 %fusion = (f32[2,512]{1,0:T(2,128)S(1)}, f32[4608,512,2]{1,0,2:T(8,128)S(1)}) fusion(pred[512,4608]{0,1:T(8,128)(4,1)S(1)} %fusion.10, f32[512,2,64]{2,0,1:T(8,128)S(1)} %get-tuple-element.39, f32[512,2,64]{2,0,1:T(8,128)S(1)} %get-tuple-element.38, bf16[4608,1,128]{0,2,1:T(8,128)(2,1)S(1)} %constant_dynamic-update-slice_fusion.9), kind=kOutput, calls=%fused_computation.3 | convolution fusion | flops 1227226112 | bytes 22941696 | tf_op jit(solution)/shard_map/while/body/eval_jaxpr/qgrd,kgd->grqk/dot_general | solution.py:101
  348.1 6.3 %fusion.24 = bf16[512,1,2,128]{0,3,2,1:T(8,128)(2,1)S(1)} fusion(f32[4608,512,2]{1,0,2:T(8,128)S(1)} %get-tuple-element.59, pred[512,4608]{0,1:T(8,128)(4,1)S(1)} %fusion.10, bf16[4608,1,128]{2,0,1:T(8,128)(2,1)S(1)} %constant_dynamic-update-slice_fusion, f32[512,2]{0,1:T(2,128)S(1)} %bitcast.95), kind=kOutput, calls=%fused_computation.26 | convolution fusion | flops 1227096064 | bytes 22679552 | tf_op jit(solution)/shard_map/while/body/eval_jaxpr/grqk,kgd->qgrd/dot_general | solution.py:106
  354.5 37.5 %all-gather.14.cloned.1.call-done = bf16[256,4608]{0,1:T(8,128)(2,1)} async-done(((bf16[256,288]{0,1:T(8,128)(2,1)}), bf16[256,4608]{0,1:T(8,128)(2,1)}) %all-gather.14.cloned.1.call-update) | async-done | bytes 2359312 | tf_op jit(solution)/shard_map/all_gather | solution.py:116
  391.9 5.2 %convolution_convert_fusion = bf16[512,4608]{0,1:T(8,128)(2,1)} fusion(bf16[256,4608]{0,1:T(8,128)(2,1)} %all-gather.14.cloned.1.call-done, bf16[512,256]{0,1:T(8,128)(2,1)S(1)} %bitcast.94), kind=kOutput, calls=%fused_computation.16 | convolution fusion | flops 1210318848 | bytes 7340032 | tf_op jit(solution)/shard_map/dot_general | solution.py:114
  397.2 0.6 copy-done.23
  398.3 0.4 fusion.18
  398.8 0.7 copy.21
  399.4 0.7 copy.20
  400.1 67.7 %reduce-scatter.2.cloned.1.call-done = bf16[512,288]{0,1:T(8,128)(2,1)} async-done(((bf16[512,4608]{0,1:T(8,128)(2,1)}), bf16[512,288]{0,1:T(8,128)(2,1)}) %reduce-scatter.2.cloned.1.call-update) | async-done | bytes 294928 | tf_op jit(solution)/shard_map/reduce_scatter | solution.py:119
  467.8 1.1 fusion.29
  468.9 29.2 %psum.7 = f32[512]{0:T(512)S(1)} all-reduce(f32[512]{0:T(512)S(1)} %fusion.29), channel_id=1, replica_groups=mesh['seq'=16,'mp'=16] {'mp'}, use_global_device_ids=true, to_apply=%region_9.10 | all-reduce | flops 512 | bytes 4096 | tf_op jit(solution)/shard_map/psum | solution.py:123
  498.0 1.8 fusion.32
  (97 shorter events, 1.4 us)
Async XLA Ops:
  7.2 85.3 %all-gather.6.cloned.1.call-start = ((), (), s32[]{:S(2)}) async-start(), calls=%async_computation.1 | async-start | bytes 5013504 | tf_op jit(solution)/shard_map/all_gather | solution.py:46
  7.9 127.3 %all-gather.10.cloned.1.call-start = ((), (), s32[]{:S(2)}) async-start(), calls=%async_computation.3 | async-start | bytes 1253376 | tf_op jit(solution)/shard_map/all_gather | solution.py:55
  8.6 205.7 %all-gather.8.cloned.1.call-start = ((), (), s32[]{:S(2)}) async-start(), calls=%async_computation.2 | async-start | bytes 1253376 | tf_op jit(solution)/shard_map/all_gather | solution.py:56
  9.4 295.1 %all-gather.12.cloned.1.call-start = ((), (), s32[]{:S(2)}) async-start(), calls=%async_computation.4 | async-start | bytes 2506752 | tf_op jit(solution)/shard_map/all_gather | solution.py:54
  10.0 382.0 %all-gather.14.cloned.1.call-start = ((), (), s32[]{:S(2)}) async-start(), calls=%async_computation.5 | async-start | bytes 2506752 | tf_op jit(solution)/shard_map/all_gather | solution.py:116
  140.2 107.1 %copy-start.21 = (s32[512]{0:T(512)S(1)}, s32[512]{0:T(512)}, u32[]{:S(2)}) copy-start(s32[512]{0:T(512)} %param.16) | copy-start | bytes 6148
  140.2 81.4 %collective-permute-start.8 = (bf16[512,1,128]{0,2,1:T(8,128)(2,1)S(1)}, bf16[512,1,128]{0,2,1:T(8,128)(2,1)S(1)}, u32[]{:S(2)}, u32[]{:S(2)}) collective-permute-start(bf16[512,1,128]{0,2,1:T(8,128)(2,1)S(1)} %pad_maximum_fusion), channel_id=1, source_target_pairs={{0,16},{16,32},{32,48},{48,64},{64,80},{80,96},{96,112},{112,128},... | collective-permute-start | bytes 393224 | tf_op jit(solution)/shard_map/ppermute | solution.py:21
  219.2 28.1 %copy-start.1 = (bf16[512,128]{1,0:T(8,128)(2,1)}, bf16[512,128]{1,0:T(8,128)(2,1)S(1)}, u32[]{:S(2)}) copy-start(bf16[512,128]{1,0:T(8,128)(2,1)S(1)} %convolution_convert_fusion.2) | copy-start | bytes 393220
  219.2 9.3 %collective-permute-start = (bf16[512,1,128]{2,0,1:T(8,128)(2,1)S(1)}, bf16[512,1,128]{2,0,1:T(8,128)(2,1)S(1)}, u32[]{:S(2)}, u32[]{:S(2)}) collective-permute-start(bf16[512,1,128]{2,0,1:T(8,128)(2,1)S(1)} %bitcast.92), channel_id=1, source_target_pairs={{0,16},{16,32},{32,48},{48,64},{64,80},{80,96},{96,112},{112,128},... | collective-permute-start | bytes 393224 | tf_op jit(solution)/shard_map/ppermute | solution.py:21
  221.6 25.6 %copy-start.5 = (bf16[512,1,128]{0,2,1:T(8,128)(2,1)}, bf16[512,1,128]{0,2,1:T(8,128)(2,1)S(1)}, u32[]{:S(2)}) copy-start(bf16[512,1,128]{0,2,1:T(8,128)(2,1)S(1)} %collective-permute-done.8) | copy-start | bytes 393220
  221.7 10.4 %collective-permute-start.9 = (bf16[512,1,128]{0,2,1:T(8,128)(2,1)S(1)}, bf16[512,1,128]{0,2,1:T(8,128)(2,1)S(1)}, u32[]{:S(2)}, u32[]{:S(2)}) collective-permute-start(bf16[512,1,128]{0,2,1:T(8,128)(2,1)S(1)} %collective-permute-done.8), channel_id=1, source_target_pairs={{0,16},{16,32},{32,48},{48,64},{64,80},{80,96},{96,112},{112,128},... | collective-permute-start | bytes 393224 | tf_op jit(solution)/shard_map/ppermute | solution.py:21
  227.1 240.7 %reduce-scatter.2.cloned.1.call-start = ((), (), s32[]{:S(2)}) async-start(), calls=%async_computation.6 | async-start | bytes 5013504 | tf_op jit(solution)/shard_map/reduce_scatter | solution.py:119
  228.4 18.8 %copy-start.3 = (bf16[512,1,128]{2,0,1:T(8,128)(2,1)}, bf16[512,1,128]{2,0,1:T(8,128)(2,1)S(1)}, u32[]{:S(2)}) copy-start(bf16[512,1,128]{2,0,1:T(8,128)(2,1)S(1)} %collective-permute-done) | copy-start | bytes 393220
  228.4 9.9 %collective-permute-start.1 = (bf16[512,1,128]{2,0,1:T(8,128)(2,1)S(1)}, bf16[512,1,128]{2,0,1:T(8,128)(2,1)S(1)}, u32[]{:S(2)}, u32[]{:S(2)}) collective-permute-start(bf16[512,1,128]{2,0,1:T(8,128)(2,1)S(1)} %collective-permute-done), channel_id=1, source_target_pairs={{0,16},{16,32},{32,48},{48,64},{64,80},{80,96},{96,112},{112,128},... | collective-permute-start | bytes 393224 | tf_op jit(solution)/shard_map/ppermute | solution.py:21
  232.1 39.5 %copy-start.9 = (bf16[512,1,128]{0,2,1:T(8,128)(2,1)}, bf16[512,1,128]{0,2,1:T(8,128)(2,1)S(1)}, u32[]{:S(2)}) copy-start(bf16[512,1,128]{0,2,1:T(8,128)(2,1)S(1)} %collective-permute-done.9) | copy-start | bytes 393220
  232.1 11.4 %collective-permute-start.10 = (bf16[512,1,128]{0,2,1:T(8,128)(2,1)S(1)}, bf16[512,1,128]{0,2,1:T(8,128)(2,1)S(1)}, u32[]{:S(2)}, u32[]{:S(2)}) collective-permute-start(bf16[512,1,128]{0,2,1:T(8,128)(2,1)S(1)} %collective-permute-done.9), channel_id=1, source_target_pairs={{0,16},{16,32},{32,48},{48,64},{64,80},{80,96},{96,112},{112,128},... | collective-permute-start | bytes 393224 | tf_op jit(solution)/shard_map/ppermute | solution.py:21
  238.4 33.3 %copy-start.7 = (bf16[512,1,128]{2,0,1:T(8,128)(2,1)}, bf16[512,1,128]{2,0,1:T(8,128)(2,1)S(1)}, u32[]{:S(2)}) copy-start(bf16[512,1,128]{2,0,1:T(8,128)(2,1)S(1)} %collective-permute-done.1) | copy-start | bytes 393220
  238.4 14.1 %collective-permute-start.2 = (bf16[512,1,128]{2,0,1:T(8,128)(2,1)S(1)}, bf16[512,1,128]{2,0,1:T(8,128)(2,1)S(1)}, u32[]{:S(2)}, u32[]{:S(2)}) collective-permute-start(bf16[512,1,128]{2,0,1:T(8,128)(2,1)S(1)} %collective-permute-done.1), channel_id=1, source_target_pairs={{0,16},{16,32},{32,48},{48,64},{64,80},{80,96},{96,112},{112,128},... | collective-permute-start | bytes 393224 | tf_op jit(solution)/shard_map/ppermute | solution.py:21
  243.5 28.1 %copy-start.13 = (bf16[512,1,128]{0,2,1:T(8,128)(2,1)}, bf16[512,1,128]{0,2,1:T(8,128)(2,1)S(1)}, u32[]{:S(2)}) copy-start(bf16[512,1,128]{0,2,1:T(8,128)(2,1)S(1)} %collective-permute-done.10) | copy-start | bytes 393220
  243.5 13.0 %collective-permute-start.11 = (bf16[512,1,128]{0,2,1:T(8,128)(2,1)S(1)}, bf16[512,1,128]{0,2,1:T(8,128)(2,1)S(1)}, u32[]{:S(2)}, u32[]{:S(2)}) collective-permute-start(bf16[512,1,128]{0,2,1:T(8,128)(2,1)S(1)} %collective-permute-done.10), channel_id=1, source_target_pairs={{0,16},{16,32},{32,48},{48,64},{64,80},{80,96},{96,112},{112,128},... | collective-permute-start | bytes 393224 | tf_op jit(solution)/shard_map/ppermute | solution.py:21
  252.5 19.2 %copy-start.11 = (bf16[512,1,128]{2,0,1:T(8,128)(2,1)}, bf16[512,1,128]{2,0,1:T(8,128)(2,1)S(1)}, u32[]{:S(2)}) copy-start(bf16[512,1,128]{2,0,1:T(8,128)(2,1)S(1)} %collective-permute-done.2) | copy-start | bytes 393220
  252.5 10.5 %collective-permute-start.3 = (bf16[512,1,128]{2,0,1:T(8,128)(2,1)S(1)}, bf16[512,1,128]{2,0,1:T(8,128)(2,1)S(1)}, u32[]{:S(2)}, u32[]{:S(2)}) collective-permute-start(bf16[512,1,128]{2,0,1:T(8,128)(2,1)S(1)} %collective-permute-done.2), channel_id=1, source_target_pairs={{0,16},{16,32},{32,48},{48,64},{64,80},{80,96},{96,112},{112,128},... | collective-permute-start | bytes 393224 | tf_op jit(solution)/shard_map/ppermute | solution.py:21
  256.5 52.9 %copy-start.17 = (bf16[512,1,128]{0,2,1:T(8,128)(2,1)}, bf16[512,1,128]{0,2,1:T(8,128)(2,1)S(1)}, u32[]{:S(2)}) copy-start(bf16[512,1,128]{0,2,1:T(8,128)(2,1)S(1)} %collective-permute-done.11) | copy-start | bytes 393220
  256.5 10.8 %collective-permute-start.12 = (bf16[512,1,128]{0,2,1:T(8,128)(2,1)S(1)}, bf16[512,1,128]{0,2,1:T(8,128)(2,1)S(1)}, u32[]{:S(2)}, u32[]{:S(2)}) collective-permute-start(bf16[512,1,128]{0,2,1:T(8,128)(2,1)S(1)} %collective-permute-done.11), channel_id=1, source_target_pairs={{0,16},{16,32},{32,48},{48,64},{64,80},{80,96},{96,112},{112,128},... | collective-permute-start | bytes 393224 | tf_op jit(solution)/shard_map/ppermute | solution.py:21
  263.0 46.4 %copy-start.15 = (bf16[512,1,128]{2,0,1:T(8,128)(2,1)}, bf16[512,1,128]{2,0,1:T(8,128)(2,1)S(1)}, u32[]{:S(2)}) copy-start(bf16[512,1,128]{2,0,1:T(8,128)(2,1)S(1)} %collective-permute-done.3) | copy-start | bytes 393220
  263.0 46.4 %collective-permute-start.4 = (bf16[512,1,128]{2,0,1:T(8,128)(2,1)S(1)}, bf16[512,1,128]{2,0,1:T(8,128)(2,1)}, u32[]{:S(2)}, u32[]{:S(2)}) collective-permute-start(bf16[512,1,128]{2,0,1:T(8,128)(2,1)S(1)} %collective-permute-done.3), channel_id=1, source_target_pairs={{0,16},{16,32},{32,48},{48,64},{64,80},{80,96},{96,112},{112,128},... | collective-permute-start | bytes 393224 | tf_op jit(solution)/shard_map/ppermute | solution.py:21
  267.3 42.0 %copy-start.19 = (bf16[512,1,128]{0,2,1:T(8,128)(2,1)}, bf16[512,1,128]{0,2,1:T(8,128)(2,1)S(1)}, u32[]{:S(2)}) copy-start(bf16[512,1,128]{0,2,1:T(8,128)(2,1)S(1)} %collective-permute-done.12) | copy-start | bytes 393220
  267.3 44.4 %collective-permute-start.13 = (bf16[512,1,128]{0,2,1:T(8,128)(2,1)S(1)}, bf16[512,1,128]{0,2,1:T(8,128)(2,1)}, u32[]{:S(2)}, u32[]{:S(2)}) collective-permute-start(bf16[512,1,128]{0,2,1:T(8,128)(2,1)S(1)} %collective-permute-done.12), channel_id=1, source_target_pairs={{0,16},{16,32},{32,48},{48,64},{64,80},{80,96},{96,112},{112,128},... | collective-permute-start | bytes 393224 | tf_op jit(solution)/shard_map/ppermute | solution.py:21
  309.4 9.7 %collective-permute-start.5 = (bf16[512,1,128]{2,0,1:T(8,128)(2,1)}, bf16[512,1,128]{2,0,1:T(8,128)(2,1)}, u32[]{:S(2)}, u32[]{:S(2)}) collective-permute-start(bf16[512,1,128]{2,0,1:T(8,128)(2,1)} %collective-permute-done.4), channel_id=1, source_target_pairs={{0,16},{16,32},{32,48},{48,64},{64,80},{80,96},{96,112},{112,128},... | collective-permute-start | bytes 393224 | tf_op jit(solution)/shard_map/ppermute | solution.py:21
  311.8 10.5 %collective-permute-start.14 = (bf16[512,1,128]{0,2,1:T(8,128)(2,1)}, bf16[512,1,128]{0,2,1:T(8,128)(2,1)}, u32[]{:S(2)}, u32[]{:S(2)}) collective-permute-start(bf16[512,1,128]{0,2,1:T(8,128)(2,1)} %collective-permute-done.13), channel_id=1, source_target_pairs={{0,16},{16,32},{32,48},{48,64},{64,80},{80,96},{96,112},{112,128},... | collective-permute-start | bytes 393224 | tf_op jit(solution)/shard_map/ppermute | solution.py:21
  319.0 16.0 %copy-start.20 = (bf16[512,1,128]{0,2,1:T(8,128)(2,1)S(1)}, bf16[512,1,128]{0,2,1:T(8,128)(2,1)}, u32[]{:S(2)}) copy-start(bf16[512,1,128]{0,2,1:T(8,128)(2,1)} %copy-done.19) | copy-start | bytes 393220
  319.0 16.0 %copy-start.18 = (bf16[512,1,128]{0,2,1:T(8,128)(2,1)S(1)}, bf16[512,1,128]{0,2,1:T(8,128)(2,1)}, u32[]{:S(2)}) copy-start(bf16[512,1,128]{0,2,1:T(8,128)(2,1)} %copy-done.17) | copy-start | bytes 393220
  319.0 16.0 %copy-start.14 = (bf16[512,1,128]{0,2,1:T(8,128)(2,1)S(1)}, bf16[512,1,128]{0,2,1:T(8,128)(2,1)}, u32[]{:S(2)}) copy-start(bf16[512,1,128]{0,2,1:T(8,128)(2,1)} %copy-done.13) | copy-start | bytes 393220
  319.0 16.0 %copy-start.10 = (bf16[512,1,128]{0,2,1:T(8,128)(2,1)S(1)}, bf16[512,1,128]{0,2,1:T(8,128)(2,1)}, u32[]{:S(2)}) copy-start(bf16[512,1,128]{0,2,1:T(8,128)(2,1)} %copy-done.9) | copy-start | bytes 393220
  319.0 16.0 %copy-start.6 = (bf16[512,1,128]{0,2,1:T(8,128)(2,1)S(1)}, bf16[512,1,128]{0,2,1:T(8,128)(2,1)}, u32[]{:S(2)}) copy-start(bf16[512,1,128]{0,2,1:T(8,128)(2,1)} %copy-done.5) | copy-start | bytes 393220
  319.1 10.4 %collective-permute-start.6 = (bf16[512,1,128]{2,0,1:T(8,128)(2,1)}, bf16[512,1,128]{2,0,1:T(8,128)(2,1)S(1)}, u32[]{:S(2)}, u32[]{:S(2)}) collective-permute-start(bf16[512,1,128]{2,0,1:T(8,128)(2,1)} %collective-permute-done.5), channel_id=1, source_target_pairs={{0,16},{16,32},{32,48},{48,64},{64,80},{80,96},{96,112},{112,128},... | collective-permute-start | bytes 393224 | tf_op jit(solution)/shard_map/ppermute | solution.py:21
  322.2 10.9 %collective-permute-start.15 = (bf16[512,1,128]{0,2,1:T(8,128)(2,1)}, bf16[512,1,128]{0,2,1:T(8,128)(2,1)S(1)}, u32[]{:S(2)}, u32[]{:S(2)}) collective-permute-start(bf16[512,1,128]{0,2,1:T(8,128)(2,1)} %collective-permute-done.14), channel_id=1, source_target_pairs={{0,16},{16,32},{32,48},{48,64},{64,80},{80,96},{96,112},{112,128},... | collective-permute-start | bytes 393224 | tf_op jit(solution)/shard_map/ppermute | solution.py:21
  329.4 11.8 %copy-start.16 = (bf16[512,1,128]{2,0,1:T(8,128)(2,1)S(1)}, bf16[512,1,128]{2,0,1:T(8,128)(2,1)}, u32[]{:S(2)}) copy-start(bf16[512,1,128]{2,0,1:T(8,128)(2,1)} %copy-done.15) | copy-start | bytes 393220
  329.4 11.9 %copy-start.12 = (bf16[512,1,128]{2,0,1:T(8,128)(2,1)S(1)}, bf16[512,1,128]{2,0,1:T(8,128)(2,1)}, u32[]{:S(2)}) copy-start(bf16[512,1,128]{2,0,1:T(8,128)(2,1)} %copy-done.11) | copy-start | bytes 393220
  329.4 11.9 %copy-start.8 = (bf16[512,1,128]{2,0,1:T(8,128)(2,1)S(1)}, bf16[512,1,128]{2,0,1:T(8,128)(2,1)}, u32[]{:S(2)}) copy-start(bf16[512,1,128]{2,0,1:T(8,128)(2,1)} %copy-done.7) | copy-start | bytes 393220
  329.4 11.9 %copy-start.4 = (bf16[512,1,128]{2,0,1:T(8,128)(2,1)S(1)}, bf16[512,1,128]{2,0,1:T(8,128)(2,1)}, u32[]{:S(2)}) copy-start(bf16[512,1,128]{2,0,1:T(8,128)(2,1)} %copy-done.3) | copy-start | bytes 393220
  329.4 12.0 %copy-start.2 = (bf16[512,128]{1,0:T(8,128)(2,1)S(1)}, bf16[512,128]{1,0:T(8,128)(2,1)}, u32[]{:S(2)}) copy-start(bf16[512,128]{1,0:T(8,128)(2,1)} %copy-done.1) | copy-start | bytes 393220
  329.4 9.9 %collective-permute-start.7 = (bf16[512,1,128]{2,0,1:T(8,128)(2,1)S(1)}, bf16[512,1,128]{2,0,1:T(8,128)(2,1)S(1)}, u32[]{:S(2)}, u32[]{:S(2)}) collective-permute-start(bf16[512,1,128]{2,0,1:T(8,128)(2,1)S(1)} %collective-permute-done.6), channel_id=1, source_target_pairs={{0,16},{16,32},{32,48},{48,64},{64,80},{80,96},{96,112},{112,128},... | collective-permute-start | bytes 393224 | tf_op jit(solution)/shard_map/ppermute | solution.py:21
  397.1 0.7 copy-start.23
  397.1 0.7 copy-start.22
  397.2 100.9 %copy-start = (bf16[512,288]{0,1:T(8,128)(2,1)S(1)}, bf16[512,288]{0,1:T(8,128)(2,1)}, u32[]{:S(2)}) copy-start(bf16[512,288]{0,1:T(8,128)(2,1)} %param.9) | copy-start | bytes 884740
Sparse Core Ops, SparseCore 0:
  9.8 43.6 all-gather.5
  56.1 79.0 all-gather.9
  137.8 76.4 all-gather.7
  216.7 87.6 all-gather.11
  306.9 85.0 all-gather.13
  397.3 70.4 reduce-scatter.1
where the time goes:
time: 508 us; the launch traced here: 507 us
  waiting for transfers between devices  262 us (52%)
  blocking collectives  102 us (20%)
  starting transfers between devices  60 us (12%)
  matrix products  32.7 us (6%)
  other arithmetic  23.6 us (5%)
  between operations  15.6 us (3%)
  local copies, waits for them, and re-layouts  11.4 us (2%)
    all_gather x1, waiting for transfers between devices, shards(): lax.all_gather(w_value, 'seq', axis=0, tiled=True)  71.6 us
    reduce_scatter x1, waiting for transfers between devices, shards(): lax.psum_scatter(group_terms.astype(jnp.bfloat16), 'mp', scatter_dimensio...  67.7 us
    ppermute x16, starting transfers between devices, from_behind(): return lax.ppermute(block, axis, route)  59.8 us
    unnamed x1, blocking collectives  53.1 us
    all_gather x1, waiting for transfers between devices, shards(): lax.all_gather(w_key, 'seq', axis=0, tiled=True)  39.3 us
    all_gather x1, waiting for transfers between devices, shards(): lax.all_gather(w_out, 'seq', axis=1, tiled=True)  37.5 us
    all_gather x1, waiting for transfers between devices, shards(): lax.all_gather(w_query, 'seq', axis=0, tiled=True)  32.8 us
    psum x1, blocking collectives, shards(): square_total = lax.psum(squares, 'mp')  29.2 us
  transfers between devices with their start and end apart: 22, of which 11 were waited for; matrix products, arithmetic and copies ran while one was open for 12% of the time, Pallas kernels for 0%

commit v1 on v0

--- a/solution.py
+++ b/solution.py
@@ -3,6 +3,7 @@
 import jax.numpy as jnp
 from jax import lax
 from jax.sharding import PartitionSpec as P
+from jax.lax import all_to_all, axis_size
 
 D = 4608
 HQ = 32
@@ -51,7 +52,12 @@
     normed = (x_whole * pre_scale * (1.0 + gain_full.astype(jnp.float32))[None, :]).astype(
         jnp.bfloat16
     )
-    query_raw = add_product(normed, lax.all_gather(w_query, "seq", axis=0, tiled=True))
+    query_raw = add_product(
+        normed,
+        jnp.concatenate(
+            all_to_all(jnp.stack([w_query for _ in range(axis_size("seq"))]), "seq", 0, 0), axis=0
+        ),
+    )
     key_raw = add_product(normed, lax.all_gather(w_key, "seq", axis=0, tiled=True))
     value_raw = add_product(normed, lax.all_gather(w_value, "seq", axis=0, tiled=True))
     heads_query = w_query.shape[1] // HD

time: 508 us -> 459 us (0.904)
  waiting for transfers between devices: 262 us -> 153 us
  blocking collectives: 102 us -> 143 us
  starting transfers between devices: 60 us -> 78.7 us
    pmin x1, blocking collectives: 19.3 us -> 60.7 us  [shards(): starts = lax.pmin(local_first, 'seq')]
    all_gather x1, waiting for transfers between devices: 39.3 us -> 0.01 us  [shards(): lax.all_gather(w_key, 'seq', axis=0, tiled=True)]
    all_gather x1, waiting for transfers between devices: 37.5 us -> 2.49 us  [shards(): lax.all_gather(w_out, 'seq', axis=1, tiled=True)]
    all_gather x1 -> x0, waiting for transfers between devices: 32.8 us -> none  [shards(): lax.all_gather(w_query, 'seq', axis=0, tiled=True)]
    all_to_all x0 -> x1, starting transfers between devices: none -> 11.2 us  [shards(): all_to_all(jnp.stack([w_query for _ in range(axis_size('seq'))]), 'seq',...]
    ppermute x16, starting transfers between devices: 59.8 us -> 67.3 us  [from_behind(): return lax.ppermute(block, axis, route)]
  transfers between devices with their start and end apart: 22 -> 22, of which waited for: 11 -> 10; matrix products, arithmetic and copies ran while one was open for 12% -> 13% of each run, Pallas kernels for 0% -> 0%
where the time goes in v1:
time: 459 us; the launch traced here: 458 us
  waiting for transfers between devices  153 us (33%)
  blocking collectives  143 us (31%)
  starting transfers between devices  78.7 us (17%)
  matrix products  32.4 us (7%)
  other arithmetic  22.9 us (5%)
  between operations  15 us (3%)
  local copies, waits for them, and re-layouts  13.1 us (3%)
    reduce_scatter x1, waiting for transfers between devices, shards(): lax.psum_scatter(group_terms.astype(jnp.bfloat16), 'mp', scatter_dimensio...  70.5 us
    all_gather x1, waiting for transfers between devices, shards(): lax.all_gather(w_value, 'seq', axis=0, tiled=True)  67.4 us
    ppermute x16, starting transfers between devices, from_behind(): return lax.ppermute(block, axis, route)  67.3 us
    pmin x1, blocking collectives, shards(): starts = lax.pmin(local_first, 'seq')  60.7 us
    unnamed x1, blocking collectives  53 us
    psum x1, blocking collectives, shards(): square_total = lax.psum(squares, 'mp')  29.2 us
    dot_general x3, matrix products, add_product(): return jnp.dot(normed, piece, preferred_element_type=jnp.float32)  14.2 us
    all_to_all x1, starting transfers between devices, shards(): all_to_all(jnp.stack([w_query for _ in range(axis_size('seq'))]), 'seq',...  11.2 us
  transfers between devices with their start and end apart: 22, of which 10 were waited for; matrix products, arithmetic and copies ran while one was open for 13% of the time, Pallas kernels for 0%

profile of v1, /device:TPU:32, one launch (start us, length us, event | category | flops | bytes accessed | tf_op | source)
XLA Modules:
  0.0 458.0 jit_solution(6200327272760096540)
XLA Ops:
  7.2 0.7 all-gather.5.cloned.1.call-update
  7.9 0.7 all-gather.9.cloned.1.call-update
  8.7 0.7 all-gather.7.cloned.1.call-update
  9.4 1.4 select_reduce_fusion.3
  10.8 2.6 pad_add_fusion
  13.4 2.6 stack.19
  16.1 11.2 %all-to-all-start = ((bf16[16,288,256]{2,1,0:T(8,128)(2,1)}), bf16[16,288,256]{2,1,0:T(8,128)(2,1)S(1)}, u32[]{:S(2)}, u32[]{:S(2)}) async-start(bf16[16,288,256]{2,1,0:T(8,128)(2,1)} %stack.19), calls=%async_computation | async-start | bytes 4718592 | tf_op jit(solution)/shard_map/all_to_all | solution.py:58
  27.3 60.7 %pmin.7 = s32[4]{0:T(128)S(1)} all-reduce(s32[4]{0:T(128)S(1)} %pad_add_fusion), channel_id=1, replica_groups=mesh['seq'=16,'mp'=16] {'seq'}, use_global_device_ids=true, to_apply=%region_5.6 | all-reduce | flops 4 | bytes 32 | tf_op jit(solution)/shard_map/pmin | solution.py:71
  88.0 0.6 dynamic-slice
  89.2 0.3 dynamic-update-slice
  89.5 53.0 %all-reduce = bf16[4608]{0:T(1024)(128)(2,1)S(1)} all-reduce(bf16[4608]{0:T(1024)(128)(2,1)S(1)} %dynamic-update-slice), channel_id=1, replica_groups=mesh['seq'=16,'mp'=16] {'mp'}, use_global_device_ids=true, to_apply=%add | all-reduce | flops 4608 | bytes 18432
  142.5 0.6 fusion.67
  143.1 2.5 subtract_convert_fusion
  145.6 3.4 fusion.2
  149.0 4.4 convolution_bitcast_fusion
  153.5 0.6 fusion.48
  154.1 5.7 %collective-permute-start.8 = (bf16[512,1,128]{0,2,1:T(8,128)(2,1)S(1)}, bf16[512,1,128]{0,2,1:T(8,128)(2,1)S(1)}, u32[]{:S(2)}, u32[]{:S(2)}) collective-permute-start(bf16[512,1,128]{0,2,1:T(8,128)(2,1)S(1)} %pad_maximum_fusion), channel_id=1, source_target_pairs={{0,16},{16,32},{32,48},{48,64},{64,80},{80,96},{96,112},{112,128},... | collective-permute-start | bytes 393224 | tf_op jit(solution)/shard_map/ppermute | solution.py:22
  159.7 67.4 %all-gather.7.cloned.1.call-done = bf16[4608,128]{1,0:T(8,128)(2,1)} async-done(((bf16[288,128]{1,0:T(8,128)(2,1)}), bf16[4608,128]{1,0:T(8,128)(2,1)}) %all-gather.7.cloned.1.call-update) | async-done | bytes 1179664 | tf_op jit(solution)/shard_map/all_gather | solution.py:62
  227.1 4.8 %convolution_convert_fusion.2 = bf16[512,128]{1,0:T(8,128)(2,1)S(1)} fusion(bf16[4608,128]{1,0:T(8,128)(2,1)} %all-gather.7.cloned.1.call-done, bf16[512,4608]{0,1:T(8,128)(2,1)} %all-gather.5.cloned.1.call-done, f32[4608]{0:T(1024)S(1)} %convert_add_fusion.1, f32[512]{0:T(512)S(1)} %add_rsqrt_fusion.1), kind=kOutput, calls=%fused_computation.26 | convolution fusion | flops 613482496 | bytes 6049792 | tf_op jit(solution)/shard_map/dot_general | solution.py:41
  232.0 2.5 collective-permute-start
  234.5 5.4 %collective-permute-start.9 = (bf16[512,1,128]{0,2,1:T(8,128)(2,1)S(1)}, bf16[512,1,128]{0,2,1:T(8,128)(2,1)S(1)}, u32[]{:S(2)}, u32[]{:S(2)}) collective-permute-start(bf16[512,1,128]{0,2,1:T(8,128)(2,1)S(1)} %collective-permute-done.8), channel_id=1, source_target_pairs={{0,16},{16,32},{32,48},{48,64},{64,80},{80,96},{96,112},{112,128},... | collective-permute-start | bytes 393224 | tf_op jit(solution)/shard_map/ppermute | solution.py:22
  239.9 1.3 collective-permute-done
  241.2 2.7 collective-permute-start.1
  244.0 0.2 collective-permute-done.9
  244.2 5.0 %collective-permute-start.10 = (bf16[512,1,128]{0,2,1:T(8,128)(2,1)S(1)}, bf16[512,1,128]{0,2,1:T(8,128)(2,1)S(1)}, u32[]{:S(2)}, u32[]{:S(2)}) collective-permute-start(bf16[512,1,128]{0,2,1:T(8,128)(2,1)S(1)} %collective-permute-done.9), channel_id=1, source_target_pairs={{0,16},{16,32},{32,48},{48,64},{64,80},{80,96},{96,112},{112,128},... | collective-permute-start | bytes 393224 | tf_op jit(solution)/shard_map/ppermute | solution.py:22
  249.3 1.2 collective-permute-done.1
  250.5 2.4 collective-permute-start.2
  252.9 2.0 collective-permute-done.10
  254.8 3.6 collective-permute-start.11
  258.4 1.8 convert_add_fusion
  260.3 4.3 collective-permute-start.3
  264.6 1.1 collective-permute-done.11
  265.7 3.4 collective-permute-start.12
  269.1 7.1 %fusion.10 = pred[512,4608]{0,1:T(8,128)(4,1)} fusion(s32[512]{0:T(512)S(1)} %copy-done.7, s32[4608]{0:T(1024)S(1)} %get-tuple-element.62, s32[512]{0:T(512)S(1)} %iota_add_fusion.1, s32[4608]{0:T(1024)S(1)} %get-tuple-element.61, pred[4608]{0:T(1024)(128)(4,1)S(1)} %fusion.54), kind=kLoop, calls=%fused_computation.14 | loop fusion | flops 16515072 | bytes 2404864 | tf_op jit(solution)/shard_map/while/body/eval_jaxpr/and | solution.py:102
  276.2 4.1 collective-permute-start.4
  280.3 5.7 %collective-permute-start.13 = (bf16[512,1,128]{0,2,1:T(8,128)(2,1)}, bf16[512,1,128]{0,2,1:T(8,128)(2,1)}, u32[]{:S(2)}, u32[]{:S(2)}) collective-permute-start(bf16[512,1,128]{0,2,1:T(8,128)(2,1)} %collective-permute-done.12), channel_id=1, source_target_pairs={{0,16},{16,32},{32,48},{48,64},{64,80},{80,96},{96,112},{112,128},... | collective-permute-start | bytes 393224 | tf_op jit(solution)/shard_map/ppermute | solution.py:22
  286.1 0.5 multiply_cosine_fusion
  286.6 2.5 copy.23
  289.2 3.5 collective-permute-start.5
  292.6 5.1 %collective-permute-start.14 = (bf16[512,1,128]{0,2,1:T(8,128)(2,1)}, bf16[512,1,128]{0,2,1:T(8,128)(2,1)S(1)}, u32[]{:S(2)}, u32[]{:S(2)}) collective-permute-start(bf16[512,1,128]{0,2,1:T(8,128)(2,1)} %collective-permute-done.13), channel_id=1, source_target_pairs={{0,16},{16,32},{32,48},{48,64},{64,80},{80,96},{96,112},{112,128},... | collective-permute-start | bytes 393224 | tf_op jit(solution)/shard_map/ppermute | solution.py:22
  297.8 4.9 %fusion.12 = f32[512,2,128]{0,2,1:T(8,128)S(1)} fusion(bf16[2,128,4608]{2,1,0:T(8,128)(2,1)} %bitcast.98, bf16[512,4608]{0,1:T(8,128)(2,1)} %all-gather.5.cloned.1.call-done, f32[4608]{0:T(1024)} %copy-done.6, f32[512]{0:T(512)S(1)} %add_rsqrt_fusion.1), kind=kOutput, calls=%fused_computation.17 | convolution fusion | flops 1217396736 | bytes 7622656 | tf_op jit(solution)/shard_map/dot_general | solution.py:41
  302.7 4.9 %collective-permute-start.6 = (bf16[512,1,128]{2,0,1:T(8,128)(2,1)S(1)}, bf16[512,1,128]{2,0,1:T(8,128)(2,1)S(1)}, u32[]{:S(2)}, u32[]{:S(2)}) collective-permute-start(bf16[512,1,128]{2,0,1:T(8,128)(2,1)S(1)} %collective-permute-done.5), channel_id=1, source_target_pairs={{0,16},{16,32},{32,48},{48,64},{64,80},{80,96},{96,112},{112,128},... | collective-permute-start | bytes 393224 | tf_op jit(solution)/shard_map/ppermute | solution.py:22
  307.6 3.0 collective-permute-start.15
  310.8 3.0 collective-permute-done.6
  313.8 6.1 %collective-permute-start.7 = (bf16[512,1,128]{2,0,1:T(8,128)(2,1)S(1)}, bf16[512,1,128]{2,0,1:T(8,128)(2,1)S(1)}, u32[]{:S(2)}, u32[]{:S(2)}) collective-permute-start(bf16[512,1,128]{2,0,1:T(8,128)(2,1)S(1)} %collective-permute-done.6), channel_id=1, source_target_pairs={{0,16},{16,32},{32,48},{48,64},{64,80},{80,96},{96,112},{112,128},... | collective-permute-start | bytes 393224 | tf_op jit(solution)/shard_map/ppermute | solution.py:22
  319.9 0.9 constant_dynamic-update-slice_fusion.15
  320.8 0.9 constant_dynamic-update-slice_fusion.14
  321.8 1.6 collective-permute-done.7
  323.5 0.9 constant_dynamic-update-slice_fusion.5
  324.5 0.9 constant_dynamic-update-slice_fusion.4
  325.5 6.4 %fusion = (f32[2,512]{1,0:T(2,128)S(1)}, f32[4608,512,2]{1,0,2:T(8,128)S(1)}) fusion(pred[512,4608]{0,1:T(8,128)(4,1)S(1)} %copy-done, f32[512,2,64]{0,2,1:T(8,128)S(1)} %get-tuple-element.42, f32[512,2,64]{0,2,1:T(8,128)S(1)} %get-tuple-element.41, bf16[4608,1,128]{0,2,1:T(8,128)(2,1)S(1)} %constant_dynamic-update-slice_fusion.9), kind=kOutput, calls=%fused_computation.3 | convolution fusion | flops 1227226112 | bytes 22941696 | tf_op jit(solution)/shard_map/while/body/eval_jaxpr/qgrd,kgd->grqk/dot_general | solution.py:107
  331.9 6.3 %fusion.26 = bf16[512,1,2,128]{0,3,2,1:T(8,128)(2,1)S(1)} fusion(f32[4608,512,2]{1,0,2:T(8,128)S(1)} %get-tuple-element.60, pred[512,4608]{0,1:T(8,128)(4,1)S(1)} %copy-done, bf16[4608,1,128]{2,0,1:T(8,128)(2,1)S(1)} %constant_dynamic-update-slice_fusion, f32[512,2]{0,1:T(2,128)S(1)} %bitcast.102), kind=kOutput, calls=%fused_computation.28 | convolution fusion | flops 1227096064 | bytes 22679552 | tf_op jit(solution)/shard_map/while/body/eval_jaxpr/grqk,kgd->qgrd/dot_general | solution.py:112
  338.2 2.5 all-gather.11.cloned.1.call-done
  340.7 5.2 %convolution_convert_fusion = bf16[512,4608]{0,1:T(8,128)(2,1)} fusion(bf16[256,4608]{0,1:T(8,128)(2,1)} %all-gather.11.cloned.1.call-done, bf16[512,256]{0,1:T(8,128)(2,1)S(1)} %bitcast.101), kind=kOutput, calls=%fused_computation.16 | convolution fusion | flops 1210318848 | bytes 7340032 | tf_op jit(solution)/shard_map/dot_general | solution.py:120
  345.9 0.6 copy-done.10
  346.7 0.1 copy.29
  346.8 0.1 copy.30
  347.1 0.4 fusion.20
  347.5 0.7 copy.33
  348.2 0.7 copy.32
  348.9 70.5 %reduce-scatter.2.cloned.1.call-done = bf16[512,288]{0,1:T(8,128)(2,1)} async-done(((bf16[512,4608]{0,1:T(8,128)(2,1)}), bf16[512,288]{0,1:T(8,128)(2,1)}) %reduce-scatter.2.cloned.1.call-update) | async-done | bytes 294928 | tf_op jit(solution)/shard_map/reduce_scatter | solution.py:125
  419.4 1.1 fusion.31
  420.4 29.2 %psum.7 = f32[512]{0:T(512)S(1)} all-reduce(f32[512]{0:T(512)S(1)} %fusion.31), channel_id=1, replica_groups=mesh['seq'=16,'mp'=16] {'mp'}, use_global_device_ids=true, to_apply=%region_9.10 | all-reduce | flops 512 | bytes 4096 | tf_op jit(solution)/shard_map/psum | solution.py:129
  449.6 1.8 fusion.34
  (71 shorter events, 1.0 us)
Async XLA Ops:
  7.2 138.4 %all-gather.5.cloned.1.call-start = ((), (), s32[]{:S(2)}) async-start(), calls=%async_computation.2 | async-start | bytes 5013504 | tf_op jit(solution)/shard_map/all_gather | solution.py:47
  7.9 141.1 %all-gather.9.cloned.1.call-start = ((), (), s32[]{:S(2)}) async-start(), calls=%async_computation.4 | async-start | bytes 1253376 | tf_op jit(solution)/shard_map/all_gather | solution.py:61
  8.6 218.5 %all-gather.7.cloned.1.call-start = ((), (), s32[]{:S(2)}) async-start(), calls=%async_computation.3 | async-start | bytes 1253376 | tf_op jit(solution)/shard_map/all_gather | solution.py:62
  16.1 71.9 %copy-start.11 = (u32[256]{0:T(256)S(1)}, u32[256]{0:T(256)}, u32[]{:S(2)}) copy-start(u32[256]{0:T(256)} %constant.69) | copy-start | bytes 3076
  16.1 73.2 %copy-start.9 = (bf16[288]{0:T(512)(128)(2,1)S(1)}, bf16[288]{0:T(512)(128)(2,1)}, u32[]{:S(2)}) copy-start(bf16[288]{0:T(512)(128)(2,1)} %param.10) | copy-start | bytes 1732
  16.1 270.6 %all-to-all-start = ((bf16[16,288,256]{2,1,0:T(8,128)(2,1)}), bf16[16,288,256]{2,1,0:T(8,128)(2,1)S(1)}, u32[]{:S(2)}, u32[]{:S(2)}) async-start(bf16[16,288,256]{2,1,0:T(8,128)(2,1)} %stack.19), calls=%async_computation | async-start | bytes 4718592 | tf_op jit(solution)/shard_map/all_to_all | solution.py:58
  27.3 313.5 %all-gather.11.cloned.1.call-start = ((), (), s32[]{:S(2)}) async-start(), calls=%async_computation.5 | async-start | bytes 2506752 | tf_op jit(solution)/shard_map/all_gather | solution.py:122
  145.6 81.5 %copy-start.6 = (f32[4608]{0:T(1024)}, f32[4608]{0:T(1024)S(1)}, u32[]{:S(2)}) copy-start(f32[4608]{0:T(1024)S(1)} %convert_add_fusion.1) | copy-start | bytes 55300
  154.0 115.1 %copy-start.7 = (s32[512]{0:T(512)S(1)}, s32[512]{0:T(512)}, u32[]{:S(2)}) copy-start(s32[512]{0:T(512)} %param.16) | copy-start | bytes 6148
  154.1 80.4 %collective-permute-start.8 = (bf16[512,1,128]{0,2,1:T(8,128)(2,1)S(1)}, bf16[512,1,128]{0,2,1:T(8,128)(2,1)S(1)}, u32[]{:S(2)}, u32[]{:S(2)}) collective-permute-start(bf16[512,1,128]{0,2,1:T(8,128)(2,1)S(1)} %pad_maximum_fusion), channel_id=1, source_target_pairs={{0,16},{16,32},{32,48},{48,64},{64,80},{80,96},{96,112},{112,128},... | collective-permute-start | bytes 393224 | tf_op jit(solution)/shard_map/ppermute | solution.py:22
  232.0 9.3 %collective-permute-start = (bf16[512,1,128]{2,0,1:T(8,128)(2,1)S(1)}, bf16[512,1,128]{2,0,1:T(8,128)(2,1)S(1)}, u32[]{:S(2)}, u32[]{:S(2)}) collective-permute-start(bf16[512,1,128]{2,0,1:T(8,128)(2,1)S(1)} %bitcast.99), channel_id=1, source_target_pairs={{0,16},{16,32},{32,48},{48,64},{64,80},{80,96},{96,112},{112,128},... | collective-permute-start | bytes 393224 | tf_op jit(solution)/shard_map/ppermute | solution.py:22
  234.5 9.7 %collective-permute-start.9 = (bf16[512,1,128]{0,2,1:T(8,128)(2,1)S(1)}, bf16[512,1,128]{0,2,1:T(8,128)(2,1)S(1)}, u32[]{:S(2)}, u32[]{:S(2)}) collective-permute-start(bf16[512,1,128]{0,2,1:T(8,128)(2,1)S(1)} %collective-permute-done.8), channel_id=1, source_target_pairs={{0,16},{16,32},{32,48},{48,64},{64,80},{80,96},{96,112},{112,128},... | collective-permute-start | bytes 393224 | tf_op jit(solution)/shard_map/ppermute | solution.py:22
  241.2 9.3 %collective-permute-start.1 = (bf16[512,1,128]{2,0,1:T(8,128)(2,1)S(1)}, bf16[512,1,128]{2,0,1:T(8,128)(2,1)S(1)}, u32[]{:S(2)}, u32[]{:S(2)}) collective-permute-start(bf16[512,1,128]{2,0,1:T(8,128)(2,1)S(1)} %collective-permute-done), channel_id=1, source_target_pairs={{0,16},{16,32},{32,48},{48,64},{64,80},{80,96},{96,112},{112,128},... | collective-permute-start | bytes 393224 | tf_op jit(solution)/shard_map/ppermute | solution.py:22
  244.2 10.7 %collective-permute-start.10 = (bf16[512,1,128]{0,2,1:T(8,128)(2,1)S(1)}, bf16[512,1,128]{0,2,1:T(8,128)(2,1)S(1)}, u32[]{:S(2)}, u32[]{:S(2)}) collective-permute-start(bf16[512,1,128]{0,2,1:T(8,128)(2,1)S(1)} %collective-permute-done.9), channel_id=1, source_target_pairs={{0,16},{16,32},{32,48},{48,64},{64,80},{80,96},{96,112},{112,128},... | collective-permute-start | bytes 393224 | tf_op jit(solution)/shard_map/ppermute | solution.py:22
  249.2 170.2 %reduce-scatter.2.cloned.1.call-start = ((), (), s32[]{:S(2)}) async-start(), calls=%async_computation.6 | async-start | bytes 5013504 | tf_op jit(solution)/shard_map/reduce_scatter | solution.py:125
  250.5 9.8 %collective-permute-start.2 = (bf16[512,1,128]{2,0,1:T(8,128)(2,1)S(1)}, bf16[512,1,128]{2,0,1:T(8,128)(2,1)S(1)}, u32[]{:S(2)}, u32[]{:S(2)}) collective-permute-start(bf16[512,1,128]{2,0,1:T(8,128)(2,1)S(1)} %collective-permute-done.1), channel_id=1, source_target_pairs={{0,16},{16,32},{32,48},{48,64},{64,80},{80,96},{96,112},{112,128},... | collective-permute-start | bytes 393224 | tf_op jit(solution)/shard_map/ppermute | solution.py:22
  254.8 25.5 %copy-start.2 = (bf16[512,1,128]{0,2,1:T(8,128)(2,1)}, bf16[512,1,128]{0,2,1:T(8,128)(2,1)S(1)}, u32[]{:S(2)}) copy-start(bf16[512,1,128]{0,2,1:T(8,128)(2,1)S(1)} %collective-permute-done.10) | copy-start | bytes 393220
  254.8 10.9 %collective-permute-start.11 = (bf16[512,1,128]{0,2,1:T(8,128)(2,1)S(1)}, bf16[512,1,128]{0,2,1:T(8,128)(2,1)S(1)}, u32[]{:S(2)}, u32[]{:S(2)}) collective-permute-start(bf16[512,1,128]{0,2,1:T(8,128)(2,1)S(1)} %collective-permute-done.10), channel_id=1, source_target_pairs={{0,16},{16,32},{32,48},{48,64},{64,80},{80,96},{96,112},{112,128},... | collective-permute-start | bytes 393224 | tf_op jit(solution)/shard_map/ppermute | solution.py:22
  260.3 15.9 %collective-permute-start.3 = (bf16[512,1,128]{2,0,1:T(8,128)(2,1)S(1)}, bf16[512,1,128]{2,0,1:T(8,128)(2,1)}, u32[]{:S(2)}, u32[]{:S(2)}) collective-permute-start(bf16[512,1,128]{2,0,1:T(8,128)(2,1)S(1)} %collective-permute-done.2), channel_id=1, source_target_pairs={{0,16},{16,32},{32,48},{48,64},{64,80},{80,96},{96,112},{112,128},... | collective-permute-start | bytes 393224 | tf_op jit(solution)/shard_map/ppermute | solution.py:22
  265.7 14.6 %copy-start.4 = (bf16[512,1,128]{0,2,1:T(8,128)(2,1)}, bf16[512,1,128]{0,2,1:T(8,128)(2,1)S(1)}, u32[]{:S(2)}) copy-start(bf16[512,1,128]{0,2,1:T(8,128)(2,1)S(1)} %collective-permute-done.11) | copy-start | bytes 393220
  265.7 14.6 %collective-permute-start.12 = (bf16[512,1,128]{0,2,1:T(8,128)(2,1)S(1)}, bf16[512,1,128]{0,2,1:T(8,128)(2,1)}, u32[]{:S(2)}, u32[]{:S(2)}) collective-permute-start(bf16[512,1,128]{0,2,1:T(8,128)(2,1)S(1)} %collective-permute-done.11), channel_id=1, source_target_pairs={{0,16},{16,32},{32,48},{48,64},{64,80},{80,96},{96,112},{112,128},... | collective-permute-start | bytes 393224 | tf_op jit(solution)/shard_map/ppermute | solution.py:22
  276.2 13.0 %collective-permute-start.4 = (bf16[512,1,128]{2,0,1:T(8,128)(2,1)}, bf16[512,1,128]{2,0,1:T(8,128)(2,1)}, u32[]{:S(2)}, u32[]{:S(2)}) collective-permute-start(bf16[512,1,128]{2,0,1:T(8,128)(2,1)} %collective-permute-done.3), channel_id=1, source_target_pairs={{0,16},{16,32},{32,48},{48,64},{64,80},{80,96},{96,112},{112,128},... | collective-permute-start | bytes 393224 | tf_op jit(solution)/shard_map/ppermute | solution.py:22
  280.3 12.3 %collective-permute-start.13 = (bf16[512,1,128]{0,2,1:T(8,128)(2,1)}, bf16[512,1,128]{0,2,1:T(8,128)(2,1)}, u32[]{:S(2)}, u32[]{:S(2)}) collective-permute-start(bf16[512,1,128]{0,2,1:T(8,128)(2,1)} %collective-permute-done.12), channel_id=1, source_target_pairs={{0,16},{16,32},{32,48},{48,64},{64,80},{80,96},{96,112},{112,128},... | collective-permute-start | bytes 393224 | tf_op jit(solution)/shard_map/ppermute | solution.py:22
  289.2 13.6 %collective-permute-start.5 = (bf16[512,1,128]{2,0,1:T(8,128)(2,1)}, bf16[512,1,128]{2,0,1:T(8,128)(2,1)S(1)}, u32[]{:S(2)}, u32[]{:S(2)}) collective-permute-start(bf16[512,1,128]{2,0,1:T(8,128)(2,1)} %collective-permute-done.4), channel_id=1, source_target_pairs={{0,16},{16,32},{32,48},{48,64},{64,80},{80,96},{96,112},{112,128},... | collective-permute-start | bytes 393224 | tf_op jit(solution)/shard_map/ppermute | solution.py:22
  292.6 15.0 %collective-permute-start.14 = (bf16[512,1,128]{0,2,1:T(8,128)(2,1)}, bf16[512,1,128]{0,2,1:T(8,128)(2,1)S(1)}, u32[]{:S(2)}, u32[]{:S(2)}) collective-permute-start(bf16[512,1,128]{0,2,1:T(8,128)(2,1)} %collective-permute-done.13), channel_id=1, source_target_pairs={{0,16},{16,32},{32,48},{48,64},{64,80},{80,96},{96,112},{112,128},... | collective-permute-start | bytes 393224 | tf_op jit(solution)/shard_map/ppermute | solution.py:22
  302.7 19.0 %copy-start.5 = (bf16[512,1,128]{0,2,1:T(8,128)(2,1)S(1)}, bf16[512,1,128]{0,2,1:T(8,128)(2,1)}, u32[]{:S(2)}) copy-start(bf16[512,1,128]{0,2,1:T(8,128)(2,1)} %copy-done.4) | copy-start | bytes 393220
  302.7 19.0 %copy-start.3 = (bf16[512,1,128]{0,2,1:T(8,128)(2,1)S(1)}, bf16[512,1,128]{0,2,1:T(8,128)(2,1)}, u32[]{:S(2)}) copy-start(bf16[512,1,128]{0,2,1:T(8,128)(2,1)} %copy-done.2) | copy-start | bytes 393220
  302.7 11.0 %collective-permute-start.6 = (bf16[512,1,128]{2,0,1:T(8,128)(2,1)S(1)}, bf16[512,1,128]{2,0,1:T(8,128)(2,1)S(1)}, u32[]{:S(2)}, u32[]{:S(2)}) collective-permute-start(bf16[512,1,128]{2,0,1:T(8,128)(2,1)S(1)} %collective-permute-done.5), channel_id=1, source_target_pairs={{0,16},{16,32},{32,48},{48,64},{64,80},{80,96},{96,112},{112,128},... | collective-permute-start | bytes 393224 | tf_op jit(solution)/shard_map/ppermute | solution.py:22
  307.6 12.2 %collective-permute-start.15 = (bf16[512,1,128]{0,2,1:T(8,128)(2,1)S(1)}, bf16[512,1,128]{0,2,1:T(8,128)(2,1)S(1)}, u32[]{:S(2)}, u32[]{:S(2)}) collective-permute-start(bf16[512,1,128]{0,2,1:T(8,128)(2,1)S(1)} %collective-permute-done.14), channel_id=1, source_target_pairs={{0,16},{16,32},{32,48},{48,64},{64,80},{80,96},{96,112},{112,128},... | collective-permute-start | bytes 393224 | tf_op jit(solution)/shard_map/ppermute | solution.py:22
  310.8 14.8 %copy-start = (pred[512,4608]{0,1:T(8,128)(4,1)S(1)}, pred[512,4608]{0,1:T(8,128)(4,1)}, u32[]{:S(2)}) copy-start(pred[512,4608]{0,1:T(8,128)(4,1)} %fusion.10) | copy-start | bytes 7077892
  313.8 9.7 %collective-permute-start.7 = (bf16[512,1,128]{2,0,1:T(8,128)(2,1)S(1)}, bf16[512,1,128]{2,0,1:T(8,128)(2,1)S(1)}, u32[]{:S(2)}, u32[]{:S(2)}) collective-permute-start(bf16[512,1,128]{2,0,1:T(8,128)(2,1)S(1)} %collective-permute-done.6), channel_id=1, source_target_pairs={{0,16},{16,32},{32,48},{48,64},{64,80},{80,96},{96,112},{112,128},... | collective-permute-start | bytes 393224 | tf_op jit(solution)/shard_map/ppermute | solution.py:22
  345.9 0.7 copy-start.10
  345.9 0.7 copy-start.8
  345.9 103.7 %copy-start.1 = (bf16[512,288]{0,1:T(8,128)(2,1)S(1)}, bf16[512,288]{0,1:T(8,128)(2,1)}, u32[]{:S(2)}) copy-start(bf16[512,288]{0,1:T(8,128)(2,1)} %param.9) | copy-start | bytes 884740
Sparse Core Ops, SparseCore 0:
  9.8 47.5 all-gather.4
  60.1 87.9 all-gather.8
  150.7 76.4 all-gather.6
  249.3 91.3 all-gather.10
  346.1 73.2 reduce-scatter.1
